TPU v7x, 32 devices: a whole 2x2x4 slice. The times are simulated.
32 devices in a mesh: frame: 8 (over y, x, core), chan: 4 (over z).
Axes of the slice: x: 2, y: 2, z: 4, core: 2. Of those that a mesh axis runs over, the one named last changes fastest.
Arguments:
- latent: bfloat16 [8, 512, 2560], P('frame', 'chan'), may hold values from -6 to 6
- spatial_w: bfloat16 [512, 4608], P('chan'), may hold values from -0.09375 to 0.09375
- spatial_b: float32 [512], P('chan'), may hold values from -0.5 to 0.5
- temporal_w: float32 [3, 512], P(None, 'chan'), may hold values from -3 to 3
- temporal_b: float32 [512], P('chan'), may hold values from -1 to 1
Outputs:
- decoded: bfloat16 [8, 512, 2560], P('frame', 'chan')
All inputs are finite; a program needn't handle non-finite values.
Results may differ from a plain program's by a relative error of at most 0.0048.
Values may be sent and summed in bfloat16 or wider, within the bound.
No kernel may reach another device: no remote copies, remote signals or barrier semaphores. Data moves between devices by JAX's collectives and lax.ppermute only.
A program may use at most 64 MiB of HBM per device.

v0:
```python
import jax
import jax.numpy as jnp
from jax import lax
from jax.sharding import PartitionSpec as P

W = 160


def convolve(image, filters, padding):
    return lax.conv_general_dilated(
        image,
        filters,
        (1, 1),
        padding,
        dimension_numbers=("NCHW", "OIHW", "NCHW"),
        preferred_element_type=jnp.float32,
    )


def three_taps(history, values, temporal_w, temporal_b):
    joined = jnp.concatenate([history, values], axis=0).astype(jnp.float32)
    frames = values.shape[0]
    extra = (1,) * (values.ndim - 2)
    taps = temporal_w.reshape((3, 1, temporal_w.shape[1]) + extra)
    bias = temporal_b.reshape((1, temporal_b.shape[0]) + extra)
    total = (
        bias
        + taps[0] * joined[0:frames]
        + taps[1] * joined[1 : frames + 1]
        + taps[2] * joined[2 : frames + 2]
    )
    return total.astype(jnp.bfloat16)


def shards(latent, spatial_w, spatial_b, temporal_w, temporal_b):
    frames, local_chan, pixels = latent.shape
    rows = pixels // W
    full_chan = spatial_w.shape[1] // 9
    shaped_w = spatial_w.reshape(spatial_w.shape[0], 3, 3, full_chan)
    empty = jnp.zeros((frames, spatial_w.shape[0], pixels), jnp.float32)
    piece = lax.all_gather(latent, "chan", axis=1, tiled=True)
    count = piece.shape[1]
    filters = shaped_w.transpose(0, 3, 1, 2)
    image = piece.reshape(frames, count, rows, W)
    summed = empty + convolve(image, filters, ((1, 1), (1, 1))).reshape(
        frames, spatial_w.shape[0], pixels
    )
    spatial = (summed + spatial_b[None, :, None]).astype(jnp.bfloat16)
    band_count = lax.axis_size("frame")
    banded = spatial.reshape(frames, local_chan, band_count, pixels // band_count)
    band = lax.all_to_all(banded, "frame", split_axis=2, concat_axis=0, tiled=True)
    zeros = jnp.zeros((2,) + band.shape[1:], jnp.bfloat16)
    filtered = three_taps(zeros, band, temporal_w, temporal_b)
    result = lax.all_to_all(filtered, "frame", split_axis=0, concat_axis=2, tiled=True)
    decoded = result.reshape(frames, local_chan, pixels)
    return decoded


def solution(mesh):
    placed = (P("frame", "chan", None), P("chan", None), P("chan"), P(None, "chan"), P("chan"))
    return jax.shard_map(
        shards, mesh=mesh, in_specs=placed, out_specs=P("frame", "chan", None), check_vma=False
    )
```

profile of v0, /device:TPU:0, one launch (start us, length us, event | category | flops | bytes accessed | tf_op | source)
XLA Modules:
  0.0 117.0 jit_solution(8465571282082702788)
XLA Ops:
  6.5 0.0 copy-start
  6.5 0.0 all-gather.2.cloned.1.call-start
  6.5 2.3 %copy.15 = bf16[1,128,2560]{1,2,0:T(8,128)(2,1)} copy(bf16[1,128,2560]{2,1,0:T(8,128)(2,1)} %param.5) | data formatting | bytes 1310720 | tf_op args[0]
  8.8 0.0 all-gather.2.cloned.1.call-update
  8.8 0.0 copy-done
  8.8 0.7 copy.19
  9.6 57.0 %all-gather.2.cloned.1.call-done = bf16[1,512,2560]{1,2,0:T(8,128)(2,1)} async-done(((bf16[1,128,2560]{1,2,0:T(8,128)(2,1)}), bf16[1,512,2560]{1,2,0:T(8,128)(2,1)}) %all-gather.2.cloned.1.call-update) | async-done | bytes 2621456 | tf_op jit(solution)/shard_map/all_gather | solution.py:41
  66.5 3.2 %copy.25 = bf16[512,16,1,160]{0,1,3,2:T(8,128)(2,1)S(1)} copy(bf16[512,16,1,160]{0,3,1,2:T(8,128)(2,1)} %bitcast.42) | data formatting | bytes 5242880
  69.7 0.2 pad.1.clone
  70.0 0.0 copy-start.4
  70.0 1.5 %copy.18 = bf16[512,16,1,8,21]{0,3,4,1,2:T(8,128)(2,1)S(1)} copy(bf16[512,16,1,8,21]{0,1,4,3,2:T(8,128)(2,1)S(1)} %bitcast.39) | data formatting | bytes 5505024 | tf_op jit(solution)/shard_map/conv_general_dilated | solution.py:10
  71.5 0.1 slice.29
  71.6 0.0 copy-done.4
  71.6 6.8 %fusion.9 = f32[16,8,21,128]{3,1,2,0:T(8,128)S(1)} fusion(bf16[128,3,3,512]{0,3,2,1:T(8,128)(2,1)S(1)} %bitcast.45, bf16[512,16,1,7,2]{0,3,4,1,2:T(8,128)(2,1)S(1)} %slice.29, bf16[512,16,1,8,21]{0,3,4,1,2:T(8,128)(2,1)S(1)} %copy.18, pred[8,21]{0,1:T(8,128)(4,1)S(1)} %copy-done.4), kind=kOutput, calls=%fused_computation.9 | convolution fusion | flops 3048161280 | bytes 5537960 | tf_op jit(solution)/shard_map/conv_general_dilated | solution.py:10
  78.4 0.3 copy.20
  78.6 0.1 slice_bitcast_fusion
  78.7 0.0 copy-start.2
  78.7 0.4 copy.21
  79.2 0.2 copy-done.2
  79.4 0.0 copy-start.1
  79.4 1.0 fusion.17
  80.3 3.7 %all-to-all-start = ((bf16[1,128,8,320]{1,3,0,2:T(8,128)(2,1)}), bf16[1,128,8,320]{1,3,0,2:T(8,128)(2,1)S(1)}, u32[]{:S(2)}, u32[]{:S(2)}) async-start(bf16[1,128,8,320]{1,3,0,2:T(8,128)(2,1)} %fusion.17), calls=%async_computation | async-start | bytes 1310720 | tf_op jit(solution)/shard_map/all_to_all | solution.py:51
  84.0 0.0 copy-done.1
  84.0 0.0 copy-start.3
  84.0 11.1 %all-to-all-done = bf16[1,128,8,320]{1,3,0,2:T(8,128)(2,1)S(1)} async-done(((bf16[1,128,8,320]{1,3,0,2:T(8,128)(2,1)}), bf16[1,128,8,320]{1,3,0,2:T(8,128)(2,1)S(1)}, u32[]{:S(2)}, u32[]{:S(2)}) %all-to-all-start) | async-done | bytes 655392 | tf_op jit(solution)/shard_map/all_to_all | solution.py:51
  95.1 0.1 pad_convert_fusion
  95.2 0.0 copy-done.3
  95.2 0.3 fusion.18
  95.6 13.5 %all_to_all.33 = bf16[8,128,1,320]{1,3,2,0:T(8,128)(2,1)S(1)} all-to-all(bf16[8,128,1,320]{1,3,2,0:T(8,128)(2,1)S(1)} %fusion.18), channel_id=1, replica_groups=mesh['frame'=8,'chan'=4] {'frame'}, dimensions={0} | all-to-all | bytes 1310720 | tf_op jit(solution)/shard_map/all_to_all | solution.py:54
  109.1 1.1 copy.24
  (1 shorter events, 0.0 us)
Async XLA Ops:
  6.5 2.3 %copy-start = (bf16[128,4608]{1,0:T(8,128)(2,1)S(1)}, bf16[128,4608]{1,0:T(8,128)(2,1)}, u32[]{:S(2)}) copy-start(bf16[128,4608]{1,0:T(8,128)(2,1)} %param.6) | copy-start | bytes 3538948
  6.5 60.0 %all-gather.2.cloned.1.call-start = ((), (), s32[]{:S(2)}) async-start(), calls=%async_computation.2 | async-start | bytes 3276800 | tf_op jit(solution)/shard_map/all_gather | solution.py:41
  70.0 1.6 %copy-start.4 = (pred[8,21]{0,1:T(8,128)(4,1)S(1)}, pred[8,21]{0,1:T(8,128)(4,1)}, u32[]{:S(2)}) copy-start(pred[8,21]{0,1:T(8,128)(4,1)} %constant.9) | copy-start | bytes 508
  78.7 0.7 copy-start.2
  79.4 4.6 %copy-start.1 = (f32[3,128]{1,0:T(4,128)S(1)}, f32[3,128]{1,0:T(4,128)}, u32[]{:S(2)}) copy-start(f32[3,128]{1,0:T(4,128)} %param.8) | copy-start | bytes 4612
  80.3 14.8 %all-to-all-start = ((bf16[1,128,8,320]{1,3,0,2:T(8,128)(2,1)}), bf16[1,128,8,320]{1,3,0,2:T(8,128)(2,1)S(1)}, u32[]{:S(2)}, u32[]{:S(2)}) async-start(bf16[1,128,8,320]{1,3,0,2:T(8,128)(2,1)} %fusion.17), calls=%async_computation | async-start | bytes 1310720 | tf_op jit(solution)/shard_map/all_to_all | solution.py:51
  84.0 11.2 %copy-start.3 = (f32[128]{0:T(128)S(1)}, f32[128]{0:T(128)}, u32[]{:S(2)}) copy-start(f32[128]{0:T(128)} %param.9) | copy-start | bytes 1540
Sparse Core Ops, SparseCore 0:
  8.9 57.5 all-gather.1
where the time goes:
time: 117 us
  waiting for transfers between devices  68.1 us (58%)
  blocking collectives  13.5 us (12%)
  between operations  13.5 us (12%)
  local copies, waits for them, and re-layouts  10.1 us (9%)
  matrix products  6.76 us (6%)
  starting transfers between devices  3.67 us (3%)
  other arithmetic  1.36 us (1%)
    all_gather x1, waiting for transfers between devices, shards(): piece = lax.all_gather(latent, 'chan', axis=1, tiled=True)  57 us
    all_to_all x1, blocking collectives, shards(): lax.all_to_all(filtered, 'frame', split_axis=0, concat_axis=2, tiled=True)  13.5 us
    all_to_all x1, waiting for transfers between devices, shards(): lax.all_to_all(banded, 'frame', split_axis=2, concat_axis=0, tiled=True)  11.1 us
    conv_general_dilated x1, matrix products, convolve(): lax.conv_general_dilated(image, filters, (1, 1), padding, dimension_numbe...  6.76 us
    unnamed x13, local copies, waits for them, and re-layouts  6.42 us
    all_to_all x1, starting transfers between devices, shards(): lax.all_to_all(banded, 'frame', split_axis=2, concat_axis=0, tiled=True)  3.66 us
    conv_general_dilated x5, local copies, waits for them, and re-layouts, convolve(): lax.conv_general_dilated(image, filters, (1, 1), padding, dimension_numbe...  2.37 us
  transfers between devices with their start and end apart: 2, of which 2 were waited for; matrix products, arithmetic and copies ran while one was open for 1% of the time, Pallas kernels for 0%

commit v1 on v0

--- a/solution.py
+++ b/solution.py
@@ -48,7 +48,10 @@
     spatial = (summed + spatial_b[None, :, None]).astype(jnp.bfloat16)
     band_count = lax.axis_size("frame")
     banded = spatial.reshape(frames, local_chan, band_count, pixels // band_count)
-    band = lax.all_to_all(banded, "frame", split_axis=2, concat_axis=0, tiled=True)
+    size = lax.axis_size("frame")
+    shards_2 = jnp.stack(jnp.split(banded, size, axis=2), axis=0)
+    shards_2 = lax.all_to_all(shards_2, "frame", split_axis=0, concat_axis=0)
+    band = jnp.concatenate(shards_2, axis=0)
     zeros = jnp.zeros((2,) + band.shape[1:], jnp.bfloat16)
     filtered = three_taps(zeros, band, temporal_w, temporal_b)
     result = lax.all_to_all(filtered, "frame", split_axis=0, concat_axis=2, tiled=True)

time: 117 us -> 122 us (1.043)
  local copies, waits for them, and re-layouts: 10.1 us -> 15.3 us
    unnamed x13 -> x20, local copies, waits for them, and re-layouts: 6.42 us -> 10.9 us
where the time goes in v1:
time: 122 us; the launch traced here: 121 us
  waiting for transfers between devices  68.1 us (56%)
  local copies, waits for them, and re-layouts  15.3 us (13%)
  blocking collectives  13.5 us (11%)
  between operations  13.5 us (11%)
  matrix products  6.76 us (6%)
  starting transfers between devices  3.67 us (3%)
    all_gather x1, waiting for transfers between devices, shards(): piece = lax.all_gather(latent, 'chan', axis=1, tiled=True)  57 us
    all_to_all x1, blocking collectives, shards(): lax.all_to_all(filtered, 'frame', split_axis=0, concat_axis=2, tiled=True)  13.5 us
    all_to_all x1, waiting for transfers between devices, shards(): shards_2 = lax.all_to_all(shards_2, 'frame', split_axis=0, concat_axis=0)  11.1 us
    unnamed x20, local copies, waits for them, and re-layouts  10.9 us
    conv_general_dilated x1, matrix products, convolve(): lax.conv_general_dilated(image, filters, (1, 1), padding, dimension_numbe...  6.76 us
    all_to_all x1, starting transfers between devices, shards(): shards_2 = lax.all_to_all(shards_2, 'frame', split_axis=0, concat_axis=0)  3.66 us
  transfers between devices with their start and end apart: 2, of which 2 were waited for; matrix products, arithmetic and copies ran while one was open for 1% of the time, Pallas kernels for 0%

profile of v1, /device:TPU:0, one launch (start us, length us, event | category | flops | bytes accessed | tf_op | source)
XLA Modules:
  0.0 121.3 jit_solution(1209879732025617245)
XLA Ops:
  6.5 2.3 %copy.22 = bf16[1,128,2560]{1,2,0:T(8,128)(2,1)} copy(bf16[1,128,2560]{2,1,0:T(8,128)(2,1)} %param.5) | data formatting | bytes 1310720 | tf_op args[0]
  8.8 0.0 all-gather.2.cloned.1.call-update
  8.8 0.7 copy.26
  9.6 57.0 %all-gather.2.cloned.1.call-done = bf16[1,512,2560]{1,2,0:T(8,128)(2,1)} async-done(((bf16[1,128,2560]{1,2,0:T(8,128)(2,1)}), bf16[1,512,2560]{1,2,0:T(8,128)(2,1)}) %all-gather.2.cloned.1.call-update) | async-done | bytes 2621456 | tf_op jit(solution)/shard_map/all_gather | solution.py:41
  66.5 3.2 %copy.31 = bf16[512,16,1,160]{0,1,3,2:T(8,128)(2,1)S(1)} copy(bf16[512,16,1,160]{0,3,1,2:T(8,128)(2,1)} %bitcast.66) | data formatting | bytes 5242880
  69.7 0.2 pad.1.clone
  70.0 0.0 copy-start.4
  70.0 1.5 %copy.25 = bf16[512,16,1,8,21]{0,3,4,1,2:T(8,128)(2,1)S(1)} copy(bf16[512,16,1,8,21]{0,1,4,3,2:T(8,128)(2,1)S(1)} %bitcast.63) | data formatting | bytes 5505024 | tf_op jit(solution)/shard_map/conv_general_dilated | solution.py:10
  71.5 0.1 slice.29
  71.6 6.8 %fusion.9 = f32[16,8,21,128]{3,1,2,0:T(8,128)S(1)} fusion(bf16[128,3,3,512]{0,3,2,1:T(8,128)(2,1)S(1)} %bitcast.69, bf16[512,16,1,7,2]{0,3,4,1,2:T(8,128)(2,1)S(1)} %slice.29, bf16[512,16,1,8,21]{0,3,4,1,2:T(8,128)(2,1)S(1)} %copy.25, pred[8,21]{0,1:T(8,128)(4,1)S(1)} %copy-done.4), kind=kOutput, calls=%fused_computation.9 | convolution fusion | flops 3048161280 | bytes 5537960 | tf_op jit(solution)/shard_map/conv_general_dilated | solution.py:10
  78.4 0.3 copy.27
  78.6 0.1 slice_bitcast_fusion
  78.7 0.0 copy-start.2
  78.7 0.4 copy.28
  79.2 0.2 copy-done.2
  79.4 0.1 fusion.16
  79.5 0.0 copy-start.1
  79.5 0.6 fusion.25
  80.2 0.6 fusion.24
  80.8 0.6 fusion.23
  81.4 0.6 fusion.22
  82.1 0.6 fusion.21
  82.7 0.6 fusion.20
  83.4 0.6 fusion.19
  84.0 0.6 fusion.18
  84.7 3.7 %all-to-all-start = ((bf16[8,1,128,1,320]{2,4,3,1,0:T(8,128)(2,1)}), bf16[8,1,128,1,320]{2,4,3,1,0:T(8,128)(2,1)S(1)}, u32[]{:S(2)}, u32[]{:S(2)}) async-start(bf16[8,1,128,1,320]{2,4,3,1,0:T(8,128)(2,1)} %fusion.18), calls=%async_computation | async-start | bytes 1310720 | tf_op jit(solution)/shard_map/all_to_all | solution.py:53
  88.3 0.0 copy-start.3
  88.3 11.1 %all-to-all-done = bf16[8,1,128,1,320]{2,4,3,1,0:T(8,128)(2,1)S(1)} async-done(((bf16[8,1,128,1,320]{2,4,3,1,0:T(8,128)(2,1)}), bf16[8,1,128,1,320]{2,4,3,1,0:T(8,128)(2,1)S(1)}, u32[]{:S(2)}, u32[]{:S(2)}) %all-to-all-start) | async-done | bytes 655392 | tf_op jit(solution)/shard_map/all_to_all | solution.py:53
  99.4 0.1 pad_convert_fusion
  99.6 0.3 fusion.17
  99.9 13.5 %all_to_all.20 = bf16[8,128,1,320]{1,3,2,0:T(8,128)(2,1)S(1)} all-to-all(bf16[8,128,1,320]{1,3,2,0:T(8,128)(2,1)S(1)} %fusion.17), channel_id=1, replica_groups=mesh['frame'=8,'chan'=4] {'frame'}, dimensions={0} | all-to-all | bytes 1310720 | tf_op jit(solution)/shard_map/all_to_all | solution.py:57
  113.4 1.1 copy.30
  (7 shorter events, 0.0 us)
Async XLA Ops:
  6.5 2.3 %copy-start = (bf16[128,4608]{1,0:T(8,128)(2,1)S(1)}, bf16[128,4608]{1,0:T(8,128)(2,1)}, u32[]{:S(2)}) copy-start(bf16[128,4608]{1,0:T(8,128)(2,1)} %param.6) | copy-start | bytes 3538948
  6.5 60.0 %all-gather.2.cloned.1.call-start = ((), (), s32[]{:S(2)}) async-start(), calls=%async_computation.2 | async-start | bytes 3276800 | tf_op jit(solution)/shard_map/all_gather | solution.py:41
  70.0 1.6 %copy-start.4 = (pred[8,21]{0,1:T(8,128)(4,1)S(1)}, pred[8,21]{0,1:T(8,128)(4,1)}, u32[]{:S(2)}) copy-start(pred[8,21]{0,1:T(8,128)(4,1)} %constant.9) | copy-start | bytes 508
  78.7 0.7 copy-start.2
  79.5 8.8 %copy-start.1 = (f32[3,128]{1,0:T(4,128)S(1)}, f32[3,128]{1,0:T(4,128)}, u32[]{:S(2)}) copy-start(f32[3,128]{1,0:T(4,128)} %param.8) | copy-start | bytes 4612
  84.7 14.8 %all-to-all-start = ((bf16[8,1,128,1,320]{2,4,3,1,0:T(8,128)(2,1)}), bf16[8,1,128,1,320]{2,4,3,1,0:T(8,128)(2,1)S(1)}, u32[]{:S(2)}, u32[]{:S(2)}) async-start(bf16[8,1,128,1,320]{2,4,3,1,0:T(8,128)(2,1)} %fusion.18), calls=%async_computation | async-start | bytes 1310720 | tf_op jit(solution)/shard_map/all_to_all | solution.py:53
  88.3 11.2 %copy-start.3 = (f32[128]{0:T(128)S(1)}, f32[128]{0:T(128)}, u32[]{:S(2)}) copy-start(f32[128]{0:T(128)} %param.9) | copy-start | bytes 1540
Sparse Core Ops, SparseCore 0:
  8.9 57.5 all-gather.1
